TPU v7x, 256 devices: a whole 4x4x8 slice. The times are simulated.
256 devices in a mesh: grp: 8 (over y, core), sub: 32 (over x, z).
Axes of the slice: x: 4, y: 4, z: 8, core: 2. Of those that a mesh axis runs over, the one named last changes fastest.
Arguments:
- cluster_pos: float32 [3, 4096], P(None, 'sub'), may hold values from -3 to 3
- cluster_vel: float32 [3, 4096], P(None, 'sub'), may hold values from -15 to 15
- cluster_mass: float32 [4096], P('sub'), may hold values from 3 to 60
- galaxy_pos: float32 [3, 131072], P(None, ('grp', 'sub')), may hold values from -1 to 7
- galaxy_vel: float32 [3, 131072], P(None, ('grp', 'sub')), may hold values from -3 to 3
- galaxy_kind: int32 [131072], P(('grp', 'sub')), may hold values from 0 to 3
- species_mass: float32 [4], replicated, may hold values from 10 to 80
Outputs:
- cluster_pos_out: float32 [3, 4096], P(None, 'sub')
- cluster_vel_out: float32 [3, 4096], P(None, 'sub')
- galaxy_pos_out: float32 [3, 131072], P(None, ('grp', 'sub'))
- galaxy_vel_out: float32 [3, 131072], P(None, ('grp', 'sub'))
All inputs are finite; a program needn't handle non-finite values.
Results may differ from a plain program's by a relative error of at most 0.0003.
Values sent between devices are 32-bit elements; how exact they have to be, the bound alone decides.
A program may use at most 64 MiB of HBM per device.

v0:
```python
import jax
import jax.numpy as jnp
from jax import lax
from jax.sharding import PartitionSpec as P

SUBSTEPS = 8


step_time = 0.5
bridge_soft = 0.01
cluster_soft = 0.0025
tile_limit = 524288


def pick_block(target_count, source_count):
    tile_size = target_count
    while tile_size > 1 and (
        tile_size * source_count > tile_limit or target_count % tile_size != 0
    ):
        tile_size = tile_size // 2
    return tile_size


def field(targets, sources, masses, soften):
    target_count = targets.shape[1]
    tile_size = pick_block(target_count, sources.shape[1])

    def field_one_tile(target_tile):
        separation = sources[:, None, :] - target_tile[:, :, None]
        distance = jnp.sum(separation * separation, axis=0) + soften
        inverse = lax.rsqrt(distance)
        weight = masses[None, :] * inverse * inverse * inverse
        return jnp.sum(separation * weight[None], axis=2)

    stacked = targets.reshape(3, target_count // tile_size, tile_size).transpose(1, 0, 2)
    result = lax.map(field_one_tile, stacked)
    return result.transpose(1, 0, 2).reshape(3, target_count)


def rates(target_pos, target_vel, source_pos, source_vel, masses, soften):
    target_count = target_pos.shape[1]
    tile_size = pick_block(target_count, source_pos.shape[1])

    def rates_one_tile(target_tile):
        separation = source_pos[:, None, :] - target_tile[:3, :, None]
        closing = source_vel[:, None, :] - target_tile[3:, :, None]
        distance = jnp.sum(separation * separation, axis=0) + soften
        inverse = lax.rsqrt(distance)
        weight = masses[None, :] * inverse * inverse * inverse
        radial = 3.0 * jnp.sum(separation * closing, axis=0) / distance
        acceleration = jnp.sum(separation * weight[None], axis=2)
        jerk_rate = jnp.sum((closing - radial[None] * separation) * weight[None], axis=2)
        return jnp.concatenate([acceleration, jerk_rate], axis=0)

    stacked = jnp.concatenate([target_pos, target_vel], axis=0)
    stacked = stacked.reshape(6, target_count // tile_size, tile_size).transpose(1, 0, 2)
    result = lax.map(rates_one_tile, stacked)
    return result.transpose(1, 0, 2).reshape(6, target_count)


def local(
    cluster_pos, cluster_vel, cluster_mass, galaxy_pos, galaxy_vel, galaxy_kind, species_mass
):
    star_count = cluster_pos.shape[1]
    member_count = lax.axis_size("sub")
    group_count = lax.axis_size("grp")
    total_stars = star_count * member_count
    total_bodies = galaxy_pos.shape[1] * member_count * group_count
    star_mass = cluster_mass / total_stars
    species = jnp.arange(species_mass.shape[0], dtype=jnp.int32)
    body_mass = (
        jnp.sum(
            jnp.where(galaxy_kind[None, :] == species[:, None], species_mass[:, None], 0.0), axis=0
        )
        / total_bodies
    )
    half_step = step_time / 2.0

    def kick(star_positions, body_positions):
        stacked = jnp.concatenate([star_positions, star_mass[None, :]], axis=0)
        gathered = lax.all_gather(stacked, "sub", axis=1, tiled=True)
        galaxy_push = field(body_positions, gathered[:3], gathered[3], bridge_soft)
        partial_value = field(gathered[:3], body_positions, body_mass, bridge_soft)
        summed = lax.psum(partial_value, ("grp", "sub"))
        cluster_pull = lax.dynamic_slice_in_dim(
            summed, lax.axis_index("sub") * star_count, star_count, 1
        )
        return (cluster_pull, galaxy_push)

    def evaluate(guess_pos, guess_vel):
        sources = jnp.concatenate([guess_pos, guess_vel, star_mass[None, :]], axis=0)
        target_pos, target_vel = (guess_pos, guess_vel)
        source_piece = lax.all_gather(sources, "sub", axis=1, tiled=True)
        result = rates(
            target_pos,
            target_vel,
            source_piece[:3],
            source_piece[3:6],
            source_piece[6],
            cluster_soft,
        )
        return (result[:3], result[3:])

    first_pull, first_push = kick(cluster_pos, galaxy_pos)
    star_vel = cluster_vel + half_step * first_pull
    body_vel = galaxy_vel + half_step * first_push
    body_pos = galaxy_pos + step_time * body_vel
    substep_time = step_time / SUBSTEPS
    positions, velocity = (cluster_pos, star_vel)
    acceleration, jerk_rate = evaluate(positions, velocity)
    for substep in range(SUBSTEPS):
        guess_pos = positions + substep_time * (
            velocity + substep_time * (acceleration / 2.0 + substep_time * jerk_rate / 6.0)
        )
        guess_vel = velocity + substep_time * (acceleration + substep_time * jerk_rate / 2.0)
        new_acc, new_jerk = evaluate(guess_pos, guess_vel)
        new_vel = (
            velocity
            + substep_time / 2.0 * (acceleration + new_acc)
            + substep_time * substep_time / 12.0 * (jerk_rate - new_jerk)
        )
        new_pos = (
            positions
            + substep_time / 2.0 * (velocity + new_vel)
            + substep_time * substep_time / 12.0 * (acceleration - new_acc)
        )
        positions, velocity, acceleration, jerk_rate = (new_pos, new_vel, new_acc, new_jerk)
    second_pull, second_push = kick(positions, body_pos)
    return (
        positions,
        velocity + half_step * second_pull,
        body_pos,
        body_vel + half_step * second_push,
    )


def solution(mesh):
    return jax.shard_map(
        local,
        mesh=mesh,
        in_specs=(
            P(None, "sub"),
            P(None, "sub"),
            P("sub"),
            P(None, ("grp", "sub")),
            P(None, ("grp", "sub")),
            P(("grp", "sub")),
            P(),
        ),
        out_specs=(
            P(None, "sub"),
            P(None, "sub"),
            P(None, ("grp", "sub")),
            P(None, ("grp", "sub")),
        ),
        check_vma=False,
    )
```

profile of v0, /device:TPU:1, one launch (start us, length us, event | category | flops | bytes accessed | tf_op | source)
XLA Modules:
  0.0 715.4 jit_solution(4176489332510097580)
XLA Ops:
  2.0 40.5 %all_gather.33 = f32[4,4096]{1,0:T(4,128)S(1)} all-gather(f32[4,128]{1,0:T(4,128)S(1)} %pad_maximum_fusion.10), channel_id=1, replica_groups=mesh['grp'=8,'sub'=32] {'sub'}, dimensions={1}, use_global_device_ids=true | all-gather | bytes 67584 | tf_op jit(solution)/shard_map/all_gather | solution.py:81
  43.3 14.5 %while.8 = (s32[]{:T(128)}, f32[4,3,1024]{2,1,0:T(4,128)S(1)}, f32[3,512]{1,0:T(4,128)}, f32[4,3,1024]{2,1,0:T(4,128)S(1)}, f32[512]{0:T(512)S(1)}, /*index=5*/s32[]{:T(128)}) while((s32[]{:T(128)}, f32[4,3,1024]{2,1,0:T(4,128)S(1)}, f32[3,512]{1,0:T(4,128)}, f32[4,3,1024]{2,1,0:T(4,128)S(1)}, f32[512]{0:T(512)S(1)}, ...), condition=%wide.region_4.5_spmd, body=%wide.region_1.4_spmd.sunk | while | flops 11006978 | bytes 8521833 | solution.py:36
  43.3 1.6 fusion.70
  45.6 1.2 fusion.71
  46.9 1.6 fusion.70
  49.3 1.2 fusion.71
  50.5 1.6 fusion.70
  52.9 1.2 fusion.71
  54.2 1.6 fusion.70
  56.5 1.2 fusion.71
  57.8 87.6 %psum.14 = f32[3,4096]{1,0:T(4,128)S(1)} all-reduce(f32[3,4096]{1,0:T(4,128)S(1)} %bitcast.93), channel_id=1, replica_groups=mesh['grp'=8,'sub'=32] {'grp','sub'}, use_global_device_ids=true, to_apply=%region_5.6 | all-reduce | flops 12288 | bytes 98304 | tf_op jit(solution)/shard_map/psum | solution.py:84
  145.4 31.0 %all_gather.34 = f32[7,4096]{1,0:T(8,128)S(1)} all-gather(f32[7,128]{1,0:T(8,128)S(1)} %pad_maximum_fusion.8), channel_id=1, replica_groups=mesh['grp'=8,'sub'=32] {'sub'}, dimensions={1}, use_global_device_ids=true | all-gather | bytes 118272 | tf_op jit(solution)/shard_map/all_gather | solution.py:93
  176.4 1.9 fusion.26
  179.0 2.1 fusion.27
  181.2 32.3 %all_gather.35 = f32[7,4096]{1,0:T(8,128)S(1)} all-gather(f32[7,128]{1,0:T(8,128)S(1)} %pad_maximum_fusion.7), channel_id=1, replica_groups=mesh['grp'=8,'sub'=32] {'sub'}, dimensions={1}, use_global_device_ids=true | all-gather | bytes 118272 | tf_op jit(solution)/shard_map/all_gather | solution.py:93
  213.5 2.0 fusion.31
  216.2 2.2 fusion.11
  218.4 31.8 %all_gather.36 = f32[7,4096]{1,0:T(8,128)S(1)} all-gather(f32[7,128]{1,0:T(8,128)S(1)} %pad_maximum_fusion.6), channel_id=1, replica_groups=mesh['grp'=8,'sub'=32] {'sub'}, dimensions={1}, use_global_device_ids=true | all-gather | bytes 118272 | tf_op jit(solution)/shard_map/all_gather | solution.py:93
  250.2 2.0 fusion.34
  252.9 2.2 fusion.13
  255.1 33.7 %all_gather.37 = f32[7,4096]{1,0:T(8,128)S(1)} all-gather(f32[7,128]{1,0:T(8,128)S(1)} %pad_maximum_fusion.5), channel_id=1, replica_groups=mesh['grp'=8,'sub'=32] {'sub'}, dimensions={1}, use_global_device_ids=true | all-gather | bytes 118272 | tf_op jit(solution)/shard_map/all_gather | solution.py:93
  288.9 2.0 fusion.37
  291.5 2.2 fusion.15
  293.7 30.9 %all_gather.38 = f32[7,4096]{1,0:T(8,128)S(1)} all-gather(f32[7,128]{1,0:T(8,128)S(1)} %pad_maximum_fusion.4), channel_id=1, replica_groups=mesh['grp'=8,'sub'=32] {'sub'}, dimensions={1}, use_global_device_ids=true | all-gather | bytes 118272 | tf_op jit(solution)/shard_map/all_gather | solution.py:93
  324.6 2.0 fusion.40
  327.3 2.2 fusion.17
  329.5 33.5 %all_gather.39 = f32[7,4096]{1,0:T(8,128)S(1)} all-gather(f32[7,128]{1,0:T(8,128)S(1)} %pad_maximum_fusion.3), channel_id=1, replica_groups=mesh['grp'=8,'sub'=32] {'sub'}, dimensions={1}, use_global_device_ids=true | all-gather | bytes 118272 | tf_op jit(solution)/shard_map/all_gather | solution.py:93
  363.0 2.0 fusion.43
  365.7 2.2 fusion.19
  367.9 30.7 %all_gather.40 = f32[7,4096]{1,0:T(8,128)S(1)} all-gather(f32[7,128]{1,0:T(8,128)S(1)} %pad_maximum_fusion.2), channel_id=1, replica_groups=mesh['grp'=8,'sub'=32] {'sub'}, dimensions={1}, use_global_device_ids=true | all-gather | bytes 118272 | tf_op jit(solution)/shard_map/all_gather | solution.py:93
  398.6 2.0 fusion.46
  401.3 2.2 fusion.21
  403.5 33.4 %all_gather.41 = f32[7,4096]{1,0:T(8,128)S(1)} all-gather(f32[7,128]{1,0:T(8,128)S(1)} %pad_maximum_fusion.1), channel_id=1, replica_groups=mesh['grp'=8,'sub'=32] {'sub'}, dimensions={1}, use_global_device_ids=true | all-gather | bytes 118272 | tf_op jit(solution)/shard_map/all_gather | solution.py:93
  437.0 2.0 fusion.49
  439.6 2.2 fusion.23
  441.8 31.1 %all_gather.42 = f32[7,4096]{1,0:T(8,128)S(1)} all-gather(f32[7,128]{1,0:T(8,128)S(1)} %pad_maximum_fusion), channel_id=1, replica_groups=mesh['grp'=8,'sub'=32] {'sub'}, dimensions={1}, use_global_device_ids=true | all-gather | bytes 118272 | tf_op jit(solution)/shard_map/all_gather | solution.py:93
  473.0 2.0 fusion.52
  475.6 2.2 fusion.25
  477.9 36.5 %all_gather.43 = f32[4,4096]{1,0:T(4,128)S(1)} all-gather(f32[4,128]{1,0:T(4,128)S(1)} %pad_maximum_fusion.9), channel_id=1, replica_groups=mesh['grp'=8,'sub'=32] {'sub'}, dimensions={1}, use_global_device_ids=true | all-gather | bytes 67584 | tf_op jit(solution)/shard_map/all_gather | solution.py:81
  514.4 8.5 %while.9 = (s32[]{:T(128)}, f32[4,3,128]{2,1,0:T(4,128)S(1)}, f32[3,4096]{1,0:T(4,128)S(1)}, f32[4,3,128]{2,1,0:T(4,128)S(1)}, f32[1,4096]{1,0:T(1,128)S(1)}, /*index=5*/s32[]{:T(128)}) while((s32[]{:T(128)}, f32[4,3,128]{2,1,0:T(4,128)S(1)}, f32[3,4096]{1,0:T(4,128)S(1)}, f32[4,3,128]{2,1,0:T(4,128)S(1)}, f32[1,4096]{1,0:T(1,128)S(1)}, ...), condition=%wide.region_45.46_spmd, body=%wide.region_42.45_spmd.sunk | while | flops 11009666 | bytes 8515149 | solution.py:36
  523.0 8.5 %while.11 = (s32[]{:T(128)}, f32[4,3,128]{2,1,0:T(4,128)S(1)}, f32[3,4096]{1,0:T(4,128)S(1)}, f32[4,3,128]{2,1,0:T(4,128)S(1)}, f32[1,4096]{1,0:T(1,128)S(1)}, /*index=5*/s32[]{:T(128)}) while((s32[]{:T(128)}, f32[4,3,128]{2,1,0:T(4,128)S(1)}, f32[3,4096]{1,0:T(4,128)S(1)}, f32[4,3,128]{2,1,0:T(4,128)S(1)}, f32[1,4096]{1,0:T(1,128)S(1)}, ...), condition=%wide.region_54.55_spmd, body=%wide.region_51.54_spmd.sunk | while | flops 11009666 | bytes 8515149 | solution.py:36
  532.1 10.4 %while.10 = (s32[]{:T(128)}, f32[4,3,1024]{2,1,0:T(4,128)S(1)}, f32[3,512]{1,0:T(4,128)S(1)}, f32[4,3,1024]{2,1,0:T(4,128)S(1)}, f32[512]{0:T(512)S(1)}, /*index=5*/s32[]{:T(128)}) while((s32[]{:T(128)}, f32[4,3,1024]{2,1,0:T(4,128)S(1)}, f32[3,512]{1,0:T(4,128)S(1)}, f32[4,3,1024]{2,1,0:T(4,128)S(1)}, f32[512]{0:T(512)S(1)}, ...), condition=%wide.region_49.50_spmd, body=%wide.region_46.49_spmd.sunk | while | flops 11006978 | bytes 8497229 | solution.py:36
  533.4 1.2 fusion.75
  534.7 0.9 fusion.74
  536.0 1.2 fusion.75
  538.6 1.2 fusion.75
  541.2 1.2 fusion.75
  542.5 171.9 %psum.15 = f32[3,4096]{1,0:T(4,128)S(1)} all-reduce(f32[3,4096]{1,0:T(4,128)S(1)} %bitcast.92), channel_id=1, replica_groups=mesh['grp'=8,'sub'=32] {'grp','sub'}, use_global_device_ids=true, to_apply=%region_50.51 | all-reduce | flops 12288 | bytes 98304 | tf_op jit(solution)/shard_map/psum | solution.py:84
  (150 shorter events, 32.9 us)
Async XLA Ops:
  43.2 102.1 %copy-start.6 = (f32[3,128]{1,0:T(4,128)S(1)}, f32[3,128]{1,0:T(4,128)}, u32[]{:S(2)}) copy-start(f32[3,128]{1,0:T(4,128)} %param.16) | copy-start | bytes 4612
  43.2 102.1 %copy-start.3 = (f32[3,128]{1,0:T(4,128)S(1)}, f32[3,128]{1,0:T(4,128)}, u32[]{:S(2)}) copy-start(f32[3,128]{1,0:T(4,128)} %param.15) | copy-start | bytes 4612
  44.9 0.7 copy-start
  48.6 0.7 copy-start
  52.2 0.7 copy-start
  55.8 0.7 copy-start
  475.6 38.8 %copy-start.1 = (f32[3,512]{1,0:T(4,128)S(1)}, f32[3,512]{1,0:T(4,128)}, u32[]{:S(2)}) copy-start(f32[3,512]{1,0:T(4,128)} %get-tuple-element.607) | copy-start | bytes 18436
  477.8 36.6 %copy-start.5 = (f32[3,128]{1,0:T(4,128)}, f32[3,128]{1,0:T(4,128)S(1)}, u32[]{:S(2)}) copy-start(f32[3,128]{1,0:T(4,128)S(1)} %multiply_add_fusion.2) | copy-start | bytes 4612
  514.4 8.5 %copy-start.4 = (f32[3,512]{1,0:T(4,128)S(1)}, f32[3,512]{1,0:T(4,128)}, u32[]{:S(2)}) copy-start(f32[3,512]{1,0:T(4,128)} %param.19) | copy-start | bytes 18436
  542.5 172.5 %copy-start.2 = (f32[3,512]{1,0:T(4,128)}, f32[3,512]{1,0:T(4,128)S(1)}, u32[]{:S(2)}) copy-start(f32[3,512]{1,0:T(4,128)S(1)} %get-tuple-element.610) | copy-start | bytes 18436
where the time goes:
time: 725 us; the launch traced here: 715 us
  blocking collectives  625 us (86%)
  other arithmetic  86 us (12%)
    all_gather x9, blocking collectives, evaluate(): source_piece = lax.all_gather(sources, 'sub', axis=1, tiled=True)  288 us
    psum x2, blocking collectives, kick(): summed = lax.psum(partial_value, ('grp', 'sub'))  259 us
    all_gather x2, blocking collectives, kick(): gathered = lax.all_gather(stacked, 'sub', axis=1, tiled=True)  76.9 us
    reduce_sum x8, other arithmetic, rates_one_tile(): jnp.sum((closing - radial[None] * separation) * weight[None], axis=2)  17.5 us
    reduce_sum x16, other arithmetic, field_one_tile(): distance = jnp.sum(separation * separation, axis=0) + soften  17.3 us
    reduce_sum x16, other arithmetic, field_one_tile(): return jnp.sum(separation * weight[None], axis=2)  16.5 us
    reduce_sum x8, other arithmetic, rates_one_tile(): radial = 3.0 * jnp.sum(separation * closing, axis=0) / distance  16.4 us

commit v1 on v0

v1 whole, which is shorter than its diff:
```python
import functools

import jax
import jax.numpy as jnp
from jax import lax
from jax.experimental import pallas as pl
from jax.experimental.pallas import tpu as pltpu
from jax.sharding import PartitionSpec as P

SUBSTEPS = 8
STEP_TIME = 0.5
HALF = STEP_TIME / 2.0
BRIDGE_SOFT = 0.01
CLUSTER_SOFT = 0.0025
F32 = jnp.float32
MESH = pl.DeviceIdType.MESH
LANES = 128


def columns(tile):
    pad = jnp.zeros((LANES - tile.shape[0], LANES), F32)
    return jnp.concatenate([tile, pad], axis=0).T


def kernel(
    sizes,
    cpos, cvel, cmass, gpos, gvel, gkind, species,
    opos, ovel, ogpos, ogvel,
    stars, wide, parts, landed, ring, ring_out, swap, landed2, ring2, ring2_out,
    target, acc6, accp, body, bvel, state,
    sa, ra, sr, rr, sz, rz, se, re, sr2, rr2, sg, rg,
):
    G, X, Z, NB, GB = sizes
    total_bodies = GB * LANES * G * NB
    total_stars = NB * LANES
    g, s = lax.axis_index("grp"), lax.axis_index("sub")
    x, z = s // Z, s % Z
    q = x * G + g
    team = lambda p: {"grp": p % G, "sub": (p // G) * Z + z}

    def copy(src, dst, send, recv, dev):
        return pltpu.make_async_remote_copy(
            src_ref=src, dst_ref=dst, send_sem=send, recv_sem=recv,
            device_id=dev, device_id_type=MESH,
        )

    def wait_blocks(buf, n, sem):
        part = buf.at[pl.ds(0, n)]
        pltpu.make_async_copy(part, part, sem).wait()

    barrier = pltpu.get_barrier_semaphore()

    def greet_sub(d, _):
        pl.semaphore_signal(
            barrier, inc=1, device_id={"grp": g, "sub": (s + d) % NB}, device_id_type=MESH
        )
        return 0

    def greet_team(d, _):
        gd = (g + 1 + d // X) % G
        xd = d % X
        pl.semaphore_signal(
            barrier, inc=1, device_id={"grp": gd, "sub": xd * Z + z}, device_id_type=MESH
        )
        return 0

    lax.fori_loop(1, NB, greet_sub, 0)
    lax.fori_loop(0, (G - 1) * X, greet_team, 0)

    stars[s] = jnp.concatenate(
        [cpos[...], cvel[...], cmass[...] / total_stars, jnp.zeros((1, LANES), F32)], axis=0
    )
    kinds = gkind[...]
    mass = jnp.zeros(kinds.shape, F32)
    for kind in range(species.shape[0]):
        mass = mass + jnp.where(kinds == kind, species[kind], 0.0)
    body[...] = mass / total_bodies

    def widen(positions):
        for b in range(GB):
            at = slice(b * LANES, (b + 1) * LANES)
            tile = jnp.concatenate(
                [positions[:, at], body[:, at], jnp.zeros((4, LANES), F32)], axis=0
            )
            cols = columns(tile)
            for i in range(4):
                wide[i, at, :] = jnp.broadcast_to(cols[:, i : i + 1], (LANES, LANES))

    widen(gpos[...])
    pl.semaphore_wait(barrier, (NB - 1) + (G - 1) * X)

    def send_stars(d, _):
        copy(stars.at[s], stars.at[s], sa, ra, {"grp": g, "sub": (s + d) % NB}).start()
        return 0

    lax.fori_loop(1, NB, send_stars, 0)
    wait_blocks(stars, NB - 1, ra)

    def pull(rows):
        at = [jnp.broadcast_to(r, (8, LANES)) for r in rows]

        def step(i, acc):
            here = pl.ds(pl.multiple_of(i * 8, 8), 8)
            d = [wide[c, here, :] - at[c] for c in range(3)]
            r2 = d[0] * d[0] + d[1] * d[1] + d[2] * d[2] + BRIDGE_SOFT
            inv = lax.rsqrt(r2)
            w = wide[3, here, :] * (inv * inv * inv)
            return tuple(acc[c] + w * d[c] for c in range(3))

        zero = jnp.zeros((8, LANES), F32)
        acc = lax.fori_loop(0, GB * LANES // 8, step, (zero, zero, zero), unroll=8)
        return jnp.concatenate(
            [jnp.sum(a, axis=0, keepdims=True) for a in acc] + [jnp.zeros((1, LANES), F32)], axis=0
        )

    def push(first, position_row):
        here = pl.ds(pl.multiple_of(first, 16), 16)
        at = [wide[c, here, :] for c in range(3)]

        def step(b, acc):
            d = [position_row(b, c) - at[c] for c in range(3)]
            r2 = d[0] * d[0] + d[1] * d[1] + d[2] * d[2] + BRIDGE_SOFT
            inv = lax.rsqrt(r2)
            w = stars[b, 6:7, :] * (inv * inv * inv)
            return tuple(acc[c] + w * d[c] for c in range(3))

        zero = jnp.zeros((16, LANES), F32)
        acc = lax.fori_loop(0, NB, step, (zero, zero, zero), unroll=4)
        for c in range(3):
            accp[c, here, :] = acc[c]

    def pushed():
        rows = []
        for c in range(3):
            rows.append(
                jnp.concatenate(
                    [
                        jnp.sum(accp[c, b * LANES : (b + 1) * LANES, :].T, axis=0, keepdims=True)
                        for b in range(GB)
                    ],
                    axis=1,
                )
            )
        return jnp.concatenate(rows, axis=0)

    def first_pull(b, _):
        p = (q + 1 + b) % NB
        parts[p] = pull([stars[p, c : c + 1, :] for c in range(3)])

        @pl.when(b < NB - 1)
        def _():
            copy(parts.at[p], landed.at[q], sr, rr, team(p)).start()

        return 0

    lax.fori_loop(0, NB, first_pull, 0)
    landed[q] = parts[q]
    wait_blocks(landed, NB - 1, rr)
    ring_out[...] = jnp.sum(landed[...], axis=0)

    def send_ring(d, _):
        copy(ring_out, ring.at[z], sz, rz, {"grp": g, "sub": x * Z + (z + d) % Z}).start()
        return 0

    lax.fori_loop(1, Z, send_ring, 0)
    ring[z] = ring_out[...]
    wait_blocks(ring, Z - 1, rz)
    mine = stars[q]
    state[0:3, :] = mine[0:3]
    state[3:6, :] = mine[3:6] + HALF * jnp.sum(ring[...], axis=0)[0:3]
    state[6:12, :] = jnp.zeros((6, LANES), F32)

    two = jnp.zeros((2, LANES), F32)

    def send_swap(par, rows):
        swap[par, q] = jnp.concatenate([rows, two], axis=0)

        def one(d, _):
            p = (q + d) % NB
            copy(swap.at[par, q], swap.at[par, q], se.at[par], re.at[par], team(p)).start()
            return 0

        lax.fori_loop(1, NB, one, 0)

    def wait_swap(par, sem):
        part = swap.at[par, pl.ds(0, NB - 1)]
        pltpu.make_async_copy(part, part, sem.at[par]).wait()

    def rates(par):
        def rows16(i, _):
            here = pl.ds(pl.multiple_of(i * 16, 16), 16)
            at = [target[c, here, :] for c in range(6)]

            def step(b, acc):
                d = [swap[par, b, c : c + 1, :] - at[c] for c in range(3)]
                v = [swap[par, b, c + 3 : c + 4, :] - at[c + 3] for c in range(3)]
                r2 = d[0] * d[0] + d[1] * d[1] + d[2] * d[2] + CLUSTER_SOFT
                rv = d[0] * v[0] + d[1] * v[1] + d[2] * v[2]
                inv = lax.rsqrt(r2)
                i2 = inv * inv
                w = stars[b, 6:7, :] * (inv * i2)
                u = w * (3.0 * i2 * rv)
                return tuple(acc[c] + w * d[c] for c in range(3)) + tuple(
                    acc[3 + c] + (w * v[c] - u * d[c]) for c in range(3)
                )

            zero = jnp.zeros((16, LANES), F32)
            acc = lax.fori_loop(0, NB, step, (zero,) * 6, unroll=4)
            for c in range(6):
                acc6[c, here, :] = acc[c]
            return 0

        lax.fori_loop(0, LANES // 16, rows16, 0)
        return jnp.concatenate(
            [jnp.sum(acc6[c].T, axis=0, keepdims=True) for c in range(6)], axis=0
        )

    h = STEP_TIME / SUBSTEPS

    def substep(k, _):
        par = k % 2
        first = k == 0
        xs, v, a, j = state[0:3, :], state[3:6, :], state[6:9, :], state[9:12, :]
        guess = jnp.concatenate(
            [
                xs + h * (v + h * (a / 2.0 + h * j / 6.0)),
                v + h * (a + h * j / 2.0),
            ],
            axis=0,
        )
        rows = jnp.where(first, state[0:6, :], guess)

        @pl.when(k >= 2)
        def _():
            wait_swap(par, se)

        send_swap(par, rows)
        cols = columns(jnp.concatenate([rows, two], axis=0))
        for c in range(6):
            target[c] = jnp.broadcast_to(cols[:, c : c + 1], (LANES, LANES))

        @pl.when(k < SUBSTEPS)
        def _():
            count = GB * LANES // SUBSTEPS

            def some(i, _):
                push(k * count + i * 16, lambda b, c: stars[b, c : c + 1, :])
                return 0

            lax.fori_loop(0, count // 16, some, 0)

        wait_swap(par, re)
        fresh = rates(par)
        a1, j1 = fresh[0:3], fresh[3:6]
        v1 = v + h / 2.0 * (a + a1) + h * h / 12.0 * (j - j1)
        x1 = xs + h / 2.0 * (v + v1) + h * h / 12.0 * (a - a1)
        state[0:3, :] = jnp.where(first, xs, x1)
        state[3:6, :] = jnp.where(first, v, v1)
        state[6:9, :] = a1
        state[9:12, :] = j1
        return 0

    lax.fori_loop(0, SUBSTEPS + 1, substep, 0)

    last = (SUBSTEPS + 1) % 2
    wait_swap(last, se)
    send_swap(last, state[0:6, :])

    velocity = gvel[...] + HALF * pushed()
    bvel[...] = velocity
    moved = gpos[...] + STEP_TIME * velocity
    ogpos[...] = moved
    widen(moved)
    wait_blocks(parts, NB - 1, sr)
    wait_swap(last, re)
    opos[...] = swap[last, s, 0:3, :]

    def second_pull(b, _):
        p = (s + 1 + b) % NB
        parts[p] = pull([swap[last, p, c : c + 1, :] for c in range(3)])

        @pl.when(b < NB - 1)
        def _():
            copy(parts.at[p], landed2.at[s], sr2, rr2, {"grp": g, "sub": p}).start()

        return 0

    lax.fori_loop(0, NB, second_pull, 0)
    landed2[s] = parts[s]

    def some_push(i, _):
        push(i * 16, lambda b, c: swap[last, b, c : c + 1, :])
        return 0

    count = GB * LANES // 16
    lax.fori_loop(0, count // 2, some_push, 0)
    wait_blocks(landed2, NB - 1, rr2)
    ring2_out[...] = jnp.sum(landed2[...], axis=0)

    def send_ring2(d, _):
        copy(ring2_out, ring2.at[g], sg, rg, {"grp": (g + d) % G, "sub": s}).start()
        return 0

    lax.fori_loop(1, G, send_ring2, 0)
    ring2[g] = ring2_out[...]
    lax.fori_loop(count // 2, count, some_push, 0)
    ogvel[...] = bvel[...] + HALF * pushed()
    wait_blocks(ring2, G - 1, rg)
    ovel[...] = swap[last, s, 3:6, :] + HALF * jnp.sum(ring2[...], axis=0)[0:3]

    wait_blocks(stars, NB - 1, sa)
    wait_blocks(ring, Z - 1, sz)
    wait_swap(1 - last, se)
    wait_swap(last, se)
    wait_blocks(landed2, NB - 1, sr2)
    wait_blocks(ring2, G - 1, sg)


def solution(mesh):
    G = mesh.shape["grp"]
    NB = mesh.shape["sub"]
    Z = G
    X = NB // Z

    def local(cpos, cvel, cmass, gpos, gvel, gkind, species):
        bodies = gpos.shape[1]
        GB = bodies // LANES
        vmem = pl.BlockSpec(memory_space=pltpu.VMEM)
        smem = pl.BlockSpec(memory_space=pltpu.SMEM)
        dma = pltpu.SemaphoreType.DMA
        return pl.pallas_call(
            functools.partial(kernel, (G, X, Z, NB, GB)),
            out_shape=(
                jax.ShapeDtypeStruct(cpos.shape, F32),
                jax.ShapeDtypeStruct(cpos.shape, F32),
                jax.ShapeDtypeStruct(gpos.shape, F32),
                jax.ShapeDtypeStruct(gpos.shape, F32),
            ),
            in_specs=[vmem] * 6 + [smem],
            out_specs=(vmem,) * 4,
            scratch_shapes=[
                pltpu.VMEM((NB, 8, LANES), F32),
                pltpu.VMEM((4, bodies, LANES), F32),
                pltpu.VMEM((NB, 4, LANES), F32),
                pltpu.VMEM((NB, 4, LANES), F32),
                pltpu.VMEM((Z, 4, LANES), F32),
                pltpu.VMEM((4, LANES), F32),
                pltpu.VMEM((2, NB, 8, LANES), F32),
                pltpu.VMEM((NB, 4, LANES), F32),
                pltpu.VMEM((G, 4, LANES), F32),
                pltpu.VMEM((4, LANES), F32),
                pltpu.VMEM((6, LANES, LANES), F32),
                pltpu.VMEM((6, LANES, LANES), F32),
                pltpu.VMEM((3, bodies, LANES), F32),
                pltpu.VMEM((1, bodies), F32),
                pltpu.VMEM((3, bodies), F32),
                pltpu.VMEM((16, LANES), F32),
                dma, dma, dma, dma, dma, dma,
                dma((2,)), dma((2,)),
                dma, dma, dma, dma,
            ],
            compiler_params=pltpu.CompilerParams(collective_id=0, has_side_effects=True),
        )(cpos, cvel, cmass.reshape(1, LANES), gpos, gvel, gkind.reshape(1, bodies), species)

    return jax.shard_map(
        local,
        mesh=mesh,
        in_specs=(
            P(None, "sub"),
            P(None, "sub"),
            P("sub"),
            P(None, ("grp", "sub")),
            P(None, ("grp", "sub")),
            P(("grp", "sub")),
            P(),
        ),
        out_specs=(
            P(None, "sub"),
            P(None, "sub"),
            P(None, ("grp", "sub")),
            P(None, ("grp", "sub")),
        ),
        check_vma=False,
    )
```

time: 725 us -> 141 us (0.19); the launches traced: 715 us -> 141 us
  blocking collectives: 625 us -> 0 us
  Pallas kernels: 0 us -> 137 us
  other arithmetic: 86 us -> 0 us
    all_gather x11 -> x0, blocking collectives: 365 us -> none  [the longest x9 288 us: evaluate(): source_piece = lax.all_gather(sources, 'sub', axis=1, tiled=True)]
    psum x2 -> x0, blocking collectives: 259 us -> none  [kick(): summed = lax.psum(partial_value, ('grp', 'sub'))]
    pallas_call x0 -> x1, Pallas kernels: none -> 137 us  [local(): pl.pallas_call(functools.partial(kernel, (G, X, Z, NB, GB)), out_shape=(j...]
    reduce_sum x51 -> x0, other arithmetic: 72.6 us -> none  [the longest x8 17.5 us: rates_one_tile(): jnp.sum((closing - radial[None] * separation) * weight[None], axis=2)]
    mul x24 -> x0, other arithmetic: 10 us -> none  [the longest x16 5.61 us: field_one_tile(): weight = masses[None, :] * inverse * inverse * inverse]
where the time goes in v1:
time: 141 us
  Pallas kernels  137 us (97%)
  local copies, waits for them, and re-layouts  3.15 us (2%)
    pallas_call x1, Pallas kernels, local(): pl.pallas_call(functools.partial(kernel, (G, X, Z, NB, GB)), out_shape=(j...  137 us
    unnamed x10, local copies, waits for them, and re-layouts  3.15 us

profile of v1, /device:TPU:1, one launch (start us, length us, event | category | flops | bytes accessed | tf_op | source)
XLA Modules:
  0.0 140.9 jit_solution(17546126511888398889)
XLA Ops:
  0.6 137.0 %shard_map.102 = (f32[3,128]{1,0:T(4,128)}, f32[3,128]{1,0:T(4,128)}, f32[3,512]{1,0:T(4,128)}, f32[3,512]{1,0:T(4,128)}) custom-call(f32[3,128]{1,0:T(4,128)} %cpos.1, f32[3,128]{1,0:T(4,128)} %cvel.1, f32[1,128]{1,0:T(1,128)} %bitcast.3, f32[3,512]{1,0:T(4,128)} %gpos.1, f32[3,512]{1,0:T(4,128)} %gvel.1, s32[1,512]{1,0:T(1,128)} %bitcast.2, f32[4]{0:T(128)} %species.1), custom_call_target="tpu_custom_call" | custom-call | tf_op jit(solution)/shard_map/pallas_call | solution.py:331
  137.7 0.0 copy-start.1
  137.7 0.0 copy-start.2
  137.7 1.3 copy.15
  139.0 0.0 copy-done.2
  139.0 0.6 copy.16
  139.6 0.0 copy-done.1
  139.6 0.0 copy-start
  139.6 0.6 copy.17
  140.2 0.1 copy-done
  140.3 0.6 copy.18
Async XLA Ops:
  137.7 1.9 %copy-start.1 = (f32[3,512]{1,0:T(4,128)S(1)}, f32[3,512]{1,0:T(4,128)}, u32[]{:S(2)}) copy-start(f32[3,512]{1,0:T(4,128)} %get-tuple-element.10) | copy-start | bytes 18436
  137.7 1.3 copy-start.2
  139.6 0.7 copy-start

commit v2 on v1

--- a/solution.py
+++ b/solution.py
@@ -15,6 +15,18 @@
 F32 = jnp.float32
 MESH = pl.DeviceIdType.MESH
 LANES = 128
+
+
+def ring_distance(d, n):
+    return min(d % n, (-d) % n)
+
+
+def chip_stages(X, Y):
+    stages = [[] for _ in range(X // 2 + Y // 2 + 1)]
+    for dx in range(X):
+        for dy in range(Y):
+            stages[ring_distance(dx, X) + ring_distance(dy, Y)].append((dx, dy))
+    return stages
 
 
 def columns(tile):
@@ -37,6 +49,9 @@
     x, z = s // Z, s % Z
     q = x * G + g
     team = lambda p: {"grp": p % G, "sub": (p // G) * Z + z}
+    Y, y, core = G // 2, g // 2, g % 2
+    stages = chip_stages(X, Y)
+    chip_at = lambda dx, dy: ((x + dx) % X) * G + ((y + dy) % Y) * 2
 
     def copy(src, dst, send, recv, dev):
         return pltpu.make_async_remote_copy(
@@ -89,29 +104,46 @@
     widen(gpos[...])
     pl.semaphore_wait(barrier, (NB - 1) + (G - 1) * X)
 
-    def send_stars(d, _):
-        copy(stars.at[s], stars.at[s], sa, ra, {"grp": g, "sub": (s + d) % NB}).start()
-        return 0
-
-    lax.fori_loop(1, NB, send_stars, 0)
-    wait_blocks(stars, NB - 1, ra)
-
-    def pull(rows):
-        at = [jnp.broadcast_to(r, (8, LANES)) for r in rows]
+    sub_stages = [
+        [[(dx, dz) for dx in range(X)] for dz in sorted({st, (-st) % Z})] for st in range(Z // 2 + 1)
+    ]
+    sub_at = lambda dx, dz: ((x + dx) % X) * Z + (z + dz) % Z
+
+    for st in reversed(range(len(sub_stages))):
+        for group in sub_stages[st]:
+            for dx, dz in group:
+                if (dx, dz) != (0, 0):
+                    copy(
+                        stars.at[s], stars.at[s], sa, ra.at[st],
+                        {"grp": g, "sub": sub_at(dx, dz)},
+                    ).start()
+
+    def pull(blocks):
+        n = len(blocks)
+        at = [[jnp.broadcast_to(r, (8, LANES)) for r in rows] for rows in blocks]
 
         def step(i, acc):
             here = pl.ds(pl.multiple_of(i * 8, 8), 8)
-            d = [wide[c, here, :] - at[c] for c in range(3)]
-            r2 = d[0] * d[0] + d[1] * d[1] + d[2] * d[2] + BRIDGE_SOFT
-            inv = lax.rsqrt(r2)
-            w = wide[3, here, :] * (inv * inv * inv)
-            return tuple(acc[c] + w * d[c] for c in range(3))
+            body_at = [wide[c, here, :] for c in range(4)]
+            out = []
+            for k in range(n):
+                d = [body_at[c] - at[k][c] for c in range(3)]
+                r2 = d[0] * d[0] + d[1] * d[1] + d[2] * d[2] + BRIDGE_SOFT
+                inv = lax.rsqrt(r2)
+                w = body_at[3] * (inv * inv * inv)
+                out.append(tuple(acc[k][c] + w * d[c] for c in range(3)))
+            return tuple(out)
 
         zero = jnp.zeros((8, LANES), F32)
-        acc = lax.fori_loop(0, GB * LANES // 8, step, (zero, zero, zero), unroll=8)
-        return jnp.concatenate(
-            [jnp.sum(a, axis=0, keepdims=True) for a in acc] + [jnp.zeros((1, LANES), F32)], axis=0
-        )
+        acc = lax.fori_loop(0, GB * LANES // 8, step, ((zero,) * 3,) * n, unroll=8 // n)
+        return [
+            jnp.concatenate(
+                [jnp.sum(a, axis=0, keepdims=True) for a in one]
+                + [jnp.zeros((1, LANES), F32)],
+                axis=0,
+            )
+            for one in acc
+        ]
 
     def push(first, position_row):
         here = pl.ds(pl.multiple_of(first, 16), 16)
@@ -143,17 +175,19 @@
             )
         return jnp.concatenate(rows, axis=0)
 
-    def first_pull(b, _):
-        p = (q + 1 + b) % NB
-        parts[p] = pull([stars[p, c : c + 1, :] for c in range(3)])
-
-        @pl.when(b < NB - 1)
-        def _():
-            copy(parts.at[p], landed.at[q], sr, rr, team(p)).start()
-
-        return 0
-
-    lax.fori_loop(0, NB, first_pull, 0)
+    for st, groups in enumerate(sub_stages):
+        count = sum(len(group) for group in groups) - (1 if st == 0 else 0)
+        wait_blocks(stars, count, ra.at[st])
+        for group in groups:
+            at = [sub_at(dx, dz) for dx, dz in group]
+            done = pull([[stars[p, c : c + 1, :] for c in range(3)] for p in at])
+            for p, value in zip(at, done):
+                parts[p] = value
+
+                @pl.when(p != q)
+                def _():
+                    copy(parts.at[p], landed.at[q], sr, rr, team(p)).start()
+
     landed[q] = parts[q]
     wait_blocks(landed, NB - 1, rr)
     ring_out[...] = jnp.sum(landed[...], axis=0)
@@ -174,24 +208,36 @@
 
     def send_swap(par, rows):
         swap[par, q] = jnp.concatenate([rows, two], axis=0)
-
-        def one(d, _):
-            p = (q + d) % NB
-            copy(swap.at[par, q], swap.at[par, q], se.at[par], re.at[par], team(p)).start()
-            return 0
-
-        lax.fori_loop(1, NB, one, 0)
-
-    def wait_swap(par, sem):
-        part = swap.at[par, pl.ds(0, NB - 1)]
-        pltpu.make_async_copy(part, part, sem.at[par]).wait()
-
-    def rates(par):
+        for st in reversed(range(len(stages))):
+            for dx, dy in stages[st]:
+                for dc in range(2):
+                    if (dx, dy, dc) != (0, 0, 0):
+                        p = chip_at(dx, dy) + (core + dc) % 2
+                        copy(
+                            swap.at[par, q], swap.at[par, q], se.at[par], re.at[par, st], team(p)
+                        ).start()
+
+    def wait_swap(par, sem, count):
+        part = swap.at[par, pl.ds(0, count)]
+        pltpu.make_async_copy(part, part, sem).wait()
+
+    def wait_sent(par):
+        wait_swap(par, se.at[par], NB - 1)
+
+    def wait_stage(par, st):
+        wait_swap(par, re.at[par, st], 2 * len(stages[st]) - (1 if st == 0 else 0))
+
+    def rates_stage(par, st):
+        blocks = [chip_at(dx, dy) + c for dx, dy in stages[st] for c in range(2)]
+
         def rows16(i, _):
             here = pl.ds(pl.multiple_of(i * 16, 16), 16)
             at = [target[c, here, :] for c in range(6)]
-
-            def step(b, acc):
+            if st == 0:
+                acc = [jnp.zeros((16, LANES), F32)] * 6
+            else:
+                acc = [acc6[c, here, :] for c in range(6)]
+            for b in blocks:
                 d = [swap[par, b, c : c + 1, :] - at[c] for c in range(3)]
                 v = [swap[par, b, c + 3 : c + 4, :] - at[c + 3] for c in range(3)]
                 r2 = d[0] * d[0] + d[1] * d[1] + d[2] * d[2] + CLUSTER_SOFT
@@ -200,17 +246,19 @@
                 i2 = inv * inv
                 w = stars[b, 6:7, :] * (inv * i2)
                 u = w * (3.0 * i2 * rv)
-                return tuple(acc[c] + w * d[c] for c in range(3)) + tuple(
+                acc = [acc[c] + w * d[c] for c in range(3)] + [
                     acc[3 + c] + (w * v[c] - u * d[c]) for c in range(3)
-                )
-
-            zero = jnp.zeros((16, LANES), F32)
-            acc = lax.fori_loop(0, NB, step, (zero,) * 6, unroll=4)
+                ]
             for c in range(6):
                 acc6[c, here, :] = acc[c]
             return 0
 
         lax.fori_loop(0, LANES // 16, rows16, 0)
+
+    def rates(par):
+        for st in range(len(stages)):
+            wait_stage(par, st)
+            rates_stage(par, st)
         return jnp.concatenate(
             [jnp.sum(acc6[c].T, axis=0, keepdims=True) for c in range(6)], axis=0
         )
@@ -232,7 +280,7 @@
 
         @pl.when(k >= 2)
         def _():
-            wait_swap(par, se)
+            wait_sent(par)
 
         send_swap(par, rows)
         cols = columns(jnp.concatenate([rows, two], axis=0))
@@ -249,7 +297,6 @@
 
             lax.fori_loop(0, count // 16, some, 0)
 
-        wait_swap(par, re)
         fresh = rates(par)
         a1, j1 = fresh[0:3], fresh[3:6]
         v1 = v + h / 2.0 * (a + a1) + h * h / 12.0 * (j - j1)
@@ -263,7 +310,7 @@
     lax.fori_loop(0, SUBSTEPS + 1, substep, 0)
 
     last = (SUBSTEPS + 1) % 2
-    wait_swap(last, se)
+    wait_sent(last)
     send_swap(last, state[0:6, :])
 
     velocity = gvel[...] + HALF * pushed()
@@ -272,20 +319,20 @@
     ogpos[...] = moved
     widen(moved)
     wait_blocks(parts, NB - 1, sr)
-    wait_swap(last, re)
+
+    for st, chips in enumerate(stages):
+        wait_stage(last, st)
+        for at in range(0, len(chips), 2):
+            some = [chip_at(dx, dy) + c for dx, dy in chips[at : at + 2] for c in range(2)]
+            done = pull([[swap[last, p, c : c + 1, :] for c in range(3)] for p in some])
+            for p, value in zip(some, done):
+                parts[p] = value
+
+                @pl.when(p != s)
+                def _():
+                    copy(parts.at[p], landed2.at[s], sr2, rr2, {"grp": g, "sub": p}).start()
+
     opos[...] = swap[last, s, 0:3, :]
-
-    def second_pull(b, _):
-        p = (s + 1 + b) % NB
-        parts[p] = pull([swap[last, p, c : c + 1, :] for c in range(3)])
-
-        @pl.when(b < NB - 1)
-        def _():
-            copy(parts.at[p], landed2.at[s], sr2, rr2, {"grp": g, "sub": p}).start()
-
-        return 0
-
-    lax.fori_loop(0, NB, second_pull, 0)
     landed2[s] = parts[s]
 
     def some_push(i, _):
@@ -310,8 +357,8 @@
 
     wait_blocks(stars, NB - 1, sa)
     wait_blocks(ring, Z - 1, sz)
-    wait_swap(1 - last, se)
-    wait_swap(last, se)
+    wait_sent(1 - last)
+    wait_sent(last)
     wait_blocks(landed2, NB - 1, sr2)
     wait_blocks(ring2, G - 1, sg)
 
@@ -355,8 +402,8 @@
                 pltpu.VMEM((1, bodies), F32),
                 pltpu.VMEM((3, bodies), F32),
                 pltpu.VMEM((16, LANES), F32),
-                dma, dma, dma, dma, dma, dma,
-                dma((2,)), dma((2,)),
+                dma, dma((Z // 2 + 1,)), dma, dma, dma, dma,
+                dma((2,)), dma((2, X // 2 + G // 4 + 1)),
                 dma, dma, dma, dma,
             ],
             compiler_params=pltpu.CompilerParams(collective_id=0, has_side_effects=True),

time: 141 us -> 125 us (0.89)
  Pallas kernels: 137 us -> 121 us
    pallas_call x1, Pallas kernels: 137 us -> 121 us  [local(): pl.pallas_call(functools.partial(kernel, (G, X, Z, NB, GB)), out_shape=(j...]
where the time goes in v2:
time: 125 us
  Pallas kernels  121 us (97%)
  local copies, waits for them, and re-layouts  3.15 us (3%)
    pallas_call x1, Pallas kernels, local(): pl.pallas_call(functools.partial(kernel, (G, X, Z, NB, GB)), out_shape=(j...  121 us
    unnamed x10, local copies, waits for them, and re-layouts  3.15 us

profile of v2, /device:TPU:1, one launch (start us, length us, event | category | flops | bytes accessed | tf_op | source)
XLA Modules:
  0.0 124.6 jit_solution(31594581254900441)
XLA Ops:
  0.6 120.7 %shard_map.102 = (f32[3,128]{1,0:T(4,128)}, f32[3,128]{1,0:T(4,128)}, f32[3,512]{1,0:T(4,128)}, f32[3,512]{1,0:T(4,128)}) custom-call(f32[3,128]{1,0:T(4,128)} %cpos.1, f32[3,128]{1,0:T(4,128)} %cvel.1, f32[1,128]{1,0:T(1,128)} %bitcast.3, f32[3,512]{1,0:T(4,128)} %gpos.1, f32[3,512]{1,0:T(4,128)} %gvel.1, s32[1,512]{1,0:T(1,128)} %bitcast.2, f32[4]{0:T(128)} %species.1), custom_call_target="tpu_custom_call" | custom-call | tf_op jit(solution)/shard_map/pallas_call | solution.py:378
  121.4 0.0 copy-start.1
  121.4 0.0 copy-start.2
  121.4 1.3 %copy.15 = f32[3,128]{1,0:T(4,128)} copy(f32[3,128]{1,0:T(4,128)} %get-tuple-element.8) | data formatting | bytes 3072
  122.7 0.0 copy-done.2
  122.7 0.6 copy.16
  123.3 0.0 copy-done.1
  123.3 0.0 copy-start
  123.3 0.6 copy.17
  123.9 0.1 copy-done
  124.0 0.6 copy.18
Async XLA Ops:
  121.4 1.9 %copy-start.1 = (f32[3,512]{1,0:T(4,128)S(1)}, f32[3,512]{1,0:T(4,128)}, u32[]{:S(2)}) copy-start(f32[3,512]{1,0:T(4,128)} %get-tuple-element.10) | copy-start | bytes 18436
  121.4 1.3 %copy-start.2 = (f32[3,128]{1,0:T(4,128)S(1)}, f32[3,128]{1,0:T(4,128)}, u32[]{:S(2)}) copy-start(f32[3,128]{1,0:T(4,128)} %get-tuple-element.9) | copy-start | bytes 4612
  123.3 0.7 copy-start

commit v3 on v1

v3 whole, which is shorter than its diff:
```python
import functools

import jax
import jax.numpy as jnp
from jax import lax
from jax.experimental import pallas as pl
from jax.experimental.pallas import tpu as pltpu
from jax.sharding import PartitionSpec as P

SUBSTEPS = 8
STEP_TIME = 0.5
HALF = STEP_TIME / 2.0
BRIDGE_SOFT = 0.01
CLUSTER_SOFT = 0.0025
F32 = jnp.float32
BF16 = jnp.bfloat16
MESH = pl.DeviceIdType.MESH
LANES = 128


def ring_distance(d, n):
    return min(d % n, (-d) % n)


def chip_stages(X, Y):
    stages = [[] for _ in range(X // 2 + Y // 2 + 1)]
    for dx in range(X):
        for dy in range(Y):
            stages[ring_distance(dx, X) + ring_distance(dy, Y)].append((dx, dy))
    return stages


def halves(tile):
    high = tile.astype(BF16).astype(F32)
    return high, tile - high


def columns(tile):
    pad = jnp.zeros((LANES - tile.shape[0], LANES), F32)
    return jnp.concatenate([tile, pad], axis=0).T


def kernel(
    sizes,
    cpos, cvel, cmass, gpos, gvel, gkind, species,
    opos, ovel, ogpos, ogvel,
    stars, wide, bodies, ring, ring_out, swap, owned, owned_out,
    target, feature, weights, acc3, accj, accp, body, bvel, state,
    sa, ra, sb, rb, sz, rz, se, re, so, ro,
):
    G, X, Z, NB, GB = sizes
    total_bodies = GB * LANES * G * NB
    total_stars = NB * LANES
    g, s = lax.axis_index("grp"), lax.axis_index("sub")
    x, z = s // Z, s % Z
    q = x * G + g
    team = lambda p: {"grp": p % G, "sub": (p // G) * Z + z}
    Y, y, core = G // 2, g // 2, g % 2
    stages = chip_stages(X, Y)
    chip_at = lambda dx, dy: ((x + dx) % X) * G + ((y + dy) % Y) * 2

    def copy(src, dst, send, recv, dev):
        return pltpu.make_async_remote_copy(
            src_ref=src, dst_ref=dst, send_sem=send, recv_sem=recv,
            device_id=dev, device_id_type=MESH,
        )

    def wait_blocks(buf, n, sem):
        part = buf.at[pl.ds(0, n)]
        pltpu.make_async_copy(part, part, sem).wait()

    barrier = pltpu.get_barrier_semaphore()

    def greet_sub(d, _):
        pl.semaphore_signal(
            barrier, inc=1, device_id={"grp": g, "sub": (s + d) % NB}, device_id_type=MESH
        )
        return 0

    def greet_team(d, _):
        gd = (g + 1 + d // X) % G
        xd = d % X
        pl.semaphore_signal(
            barrier, inc=1, device_id={"grp": gd, "sub": xd * Z + z}, device_id_type=MESH
        )
        return 0

    for zs in range(Z):

        @pl.when((g != z) | (z != zs))
        def _():
            pl.semaphore_signal(
                barrier, inc=1, device_id={"grp": z, "sub": x * Z + zs}, device_id_type=MESH
            )

    lax.fori_loop(1, NB, greet_sub, 0)
    lax.fori_loop(0, (G - 1) * X, greet_team, 0)

    stars[s] = jnp.concatenate(
        [cpos[...], cmass[...] / total_stars, cvel[...], jnp.zeros((1, LANES), F32)], axis=0
    )
    kinds = gkind[...]
    mass = jnp.zeros(kinds.shape, F32)
    for kind in range(species.shape[0]):
        mass = mass + jnp.where(kinds == kind, species[kind], 0.0)
    body[...] = mass / total_bodies

    bodies[0, q] = jnp.concatenate([gpos[...], body[...]], axis=0)

    def widen(positions):
        for b in range(GB):
            cols = columns(positions[:, b * LANES : (b + 1) * LANES])
            for i in range(3):
                wide[i, b * LANES : (b + 1) * LANES, :] = jnp.broadcast_to(
                    cols[:, i : i + 1], (LANES, LANES)
                )

    swap[...] = jnp.ones(swap.shape, F32)

    own = (z == g).astype(jnp.int32)
    pl.semaphore_wait(barrier, (NB - 1) + (G - 1) * X + Z - own)

    def send_stars(dx, dz):
        to = {"grp": g, "sub": ((x + dx) % X) * Z + (z + dz) % Z}
        if dx == 0:
            copy(stars.at[s], stars.at[s], sa.at[0], ra.at[0], to).start()
        else:
            half = stars.at[s, pl.ds(0, 4)]
            copy(half, half, sa.at[1], ra.at[1], to).start()

    def wait_halves(sem):
        part = stars.at[pl.ds(0, (X - 1) * Z), pl.ds(0, 4)]
        pltpu.make_async_copy(part, part, sem).wait()

    def peers():
        for st in range(len(stages)):
            for dx, dy in stages[st]:
                for dc in range(2):
                    if (dx, dy, dc) != (0, 0, 0):
                        yield st, chip_at(dx, dy) + (core + dc) % 2

    def send_bodies(turn):
        for st, p in peers():
            copy(
                bodies.at[turn, q], bodies.at[turn, q], sb.at[turn], rb.at[turn, st], team(p)
            ).start()

    def wait_bodies(turn, count, sem):
        part = bodies.at[turn, pl.ds(0, count)]
        pltpu.make_async_copy(part, part, sem).wait()

    stage_size = [2 * len(chips) - (1 if st == 0 else 0) for st, chips in enumerate(stages)]

    for dz in range(1, Z):
        send_stars(0, dz)
    send_bodies(0)
    for dx in range(1, X):
        for dz in range(Z):
            send_stars(dx, dz)

    def set_position(rows):
        cols = columns(rows)
        for c in range(3):
            target[c] = jnp.broadcast_to(cols[:, c : c + 1], (LANES, LANES))

    def pull(at, acc, row):
        for i in range(len(row)):
            d = [row[i][c] - at[c] for c in range(3)]
            r2 = d[0] * d[0] + d[1] * d[1] + d[2] * d[2] + BRIDGE_SOFT
            inv = lax.rsqrt(r2)
            w = row[i][3] * (inv * inv * inv)
            acc = tuple(acc[c] + w * d[c] for c in range(3))
        return acc

    def pull_rows(body_of, first):
        def rows32(i, _):
            here = pl.ds(pl.multiple_of(i * 32, 32), 32)
            at = [target[c, here, :] for c in range(3)]
            if first:
                acc = (jnp.zeros((32, LANES), F32),) * 3
            else:
                acc = tuple(acc3[c, here, :] for c in range(3))
            acc = body_of(at, acc)
            for c in range(3):
                acc3[c, here, :] = acc[c]
            return 0

        lax.fori_loop(0, LANES // 32, rows32, 0)

    def lanes_of(turn, b, l):
        return [bodies[turn, b, c : c + 1, pl.ds(l * LANES, LANES)] for c in range(4)]

    def pull_stage(turn, st):
        blocks = [chip_at(dx, dy) + c for dx, dy in stages[st] for c in range(2)]

        def some(at, acc):
            def lane(l, acc):
                l = pl.multiple_of(l * LANES, LANES)
                rows = [
                    [bodies[turn, b, c : c + 1, pl.ds(l, LANES)] for c in range(4)] for b in blocks
                ]
                return pull(at, acc, rows)

            return lax.fori_loop(0, GB, lane, acc)

        pull_rows(some, st == 0)

    def pull_all(turn):
        def some(at, acc):
            def one(b, acc):
                return pull(at, acc, [lanes_of(turn, b, l) for l in range(GB)])

            return lax.fori_loop(0, NB, one, acc)

        pull_rows(some, True)

    def pulled():
        return jnp.concatenate(
            [jnp.sum(acc3[c].T, axis=0, keepdims=True) for c in range(3)]
            + [jnp.zeros((1, LANES), F32)],
            axis=0,
        )

    def push(first, position_row):
        here = pl.ds(pl.multiple_of(first, 16), 16)
        at = [wide[c, here, :] for c in range(3)]

        def step(b, acc):
            d = [position_row(b, c) - at[c] for c in range(3)]
            r2 = d[0] * d[0] + d[1] * d[1] + d[2] * d[2] + BRIDGE_SOFT
            inv = lax.rsqrt(r2)
            w = stars[b, 3:4, :] * (inv * inv * inv)
            return tuple(acc[c] + w * d[c] for c in range(3))

        zero = jnp.zeros((16, LANES), F32)
        acc = lax.fori_loop(0, NB, step, (zero, zero, zero), unroll=4)
        for c in range(3):
            accp[c, here, :] = acc[c]

    def pushed():
        rows = []
        for c in range(3):
            rows.append(
                jnp.concatenate(
                    [
                        jnp.sum(accp[c, b * LANES : (b + 1) * LANES, :].T, axis=0, keepdims=True)
                        for b in range(GB)
                    ],
                    axis=1,
                )
            )
        return jnp.concatenate(rows, axis=0)

    widen(gpos[...])
    wait_blocks(stars, Z - 1, ra.at[0])
    set_position(stars[q, 0:3, :])
    for st in range(len(stages)):
        wait_bodies(0, stage_size[st], rb.at[0, st])
        pull_stage(0, st)
    ring_out[...] = pulled()

    def send_ring(d, _):
        copy(ring_out, ring.at[z], sz, rz, {"grp": g, "sub": x * Z + (z + d) % Z}).start()
        return 0

    lax.fori_loop(1, Z, send_ring, 0)
    ring[z] = ring_out[...]
    wait_halves(ra.at[1])
    wait_blocks(ring, Z - 1, rz)
    mine = stars[q]
    state[0:3, :] = mine[0:3]
    state[3:6, :] = mine[4:7] + HALF * jnp.sum(ring[...], axis=0)[0:3]
    state[6:12, :] = jnp.zeros((6, LANES), F32)

    one_row = jnp.ones((1, LANES), F32)
    row6 = lax.broadcasted_iota(jnp.int32, (8, LANES), 0) == 6
    none8 = jnp.zeros((8, LANES), F32)
    none16 = jnp.zeros((16, 2 * LANES), BF16)

    def dotted(rows):
        return jnp.sum(rows[0:3] * rows[3:6], axis=0, keepdims=True)

    def send_swap(par, rows):
        swap[par, q, 0:6, :] = rows
        for st, p in peers():
            copy(
                swap.at[par, q, pl.ds(0, 6)], swap.at[par, q, pl.ds(0, 6)],
                se.at[par], re.at[par, st], team(p),
            ).start()

    def wait_swap(par, sem, count):
        part = swap.at[par, pl.ds(0, count), pl.ds(0, 6)]
        pltpu.make_async_copy(part, part, sem).wait()

    def wait_sent(par):
        wait_swap(par, se.at[par], NB - 1)

    def wait_stage(par, st):
        wait_swap(par, re.at[par, st], stage_size[st])

    def set_target(rows):
        coef = jnp.concatenate([-rows[3:6], -rows[0:3], one_row, dotted(rows)], axis=0)
        high, low = halves(coef)
        cols = columns(jnp.concatenate([high, high, low, none8, rows[0:3]], axis=0))
        feature[...] = cols[:, 0:32].astype(BF16)
        for c in range(3):
            target[c] = jnp.broadcast_to(cols[:, 32 + c : 33 + c], (LANES, LANES))

    def rates_chip(par, chip, first, slot):
        sources, sums = [], []
        for k in range(2):
            tile = swap[par, chip + k]
            tile = jnp.where(row6, dotted(tile), tile)
            high, low = halves(tile)
            sources.append(jnp.concatenate([high, low, high, none8], axis=0).astype(BF16))
            high, low = halves(tile * stars[chip + k, 3:4, :])
            sums.append(jnp.concatenate([high, low], axis=0).astype(BF16))
        sums = jnp.concatenate(sums, axis=1)
        both = jnp.concatenate(
            [
                jnp.concatenate([sums, none16], axis=1),
                jnp.concatenate([none16, sums], axis=1),
            ],
            axis=0,
        )
        rv = jnp.dot(
            feature[...], jnp.concatenate(sources, axis=1), preferred_element_type=F32
        )
        for i in range(LANES // 16):
            here = slice(i * 16, (i + 1) * 16)
            at = [target[c, here, :] for c in range(3)]
            if first:
                acc = [jnp.zeros((16, LANES), F32)] * 3
            else:
                acc = [acc3[c, here, :] for c in range(3)]
            for k in range(2):
                b = chip + k
                lanes = slice(k * LANES, (k + 1) * LANES)
                d = [swap[par, b, c : c + 1, :] - at[c] for c in range(3)]
                r2 = d[0] * d[0] + d[1] * d[1] + d[2] * d[2] + CLUSTER_SOFT
                inv = lax.rsqrt(r2)
                i2 = inv * inv
                w = inv * i2
                mw = stars[b, 3:4, :] * w
                acc = [acc[c] + mw * d[c] for c in range(3)]
                weights[slot, here, lanes] = w.astype(BF16)
                u = (w * i2) * rv[here, lanes]
                weights[slot, here, 2 * LANES + k * LANES : 3 * LANES + k * LANES] = u.astype(BF16)
            for c in range(3):
                acc3[c, here, :] = acc[c]
        out = lax.dot_general(
            weights[slot], both, (((1,), (1,)), ((), ())), preferred_element_type=F32
        )
        accj[...] = out if first else accj[...] + out

    def rates(par, rows):
        turn = 0
        for st, chips in enumerate(stages):
            wait_stage(par, st)
            for dx, dy in chips:
                rates_chip(par, chip_at(dx, dy), turn == 0, turn % 2)
                turn += 1
        a = jnp.concatenate(
            [jnp.sum(acc3[c].T, axis=0, keepdims=True) for c in range(3)], axis=0
        )
        sums = jnp.concatenate([accj[...], jnp.zeros((LANES, LANES - 32), F32)], axis=1).T
        of_w = sums[0:8] + sums[8:16]
        of_u = sums[16:24] + sums[24:32]
        j = (of_w[3:6] - rows[3:6] * of_w[7:8]) - 3.0 * (of_u[0:3] - rows[0:3] * of_u[7:8])
        return jnp.concatenate([a, j], axis=0)

    h = STEP_TIME / SUBSTEPS

    def substep(k, _):
        par = k % 2
        first = k == 0
        xs, v, a, j = state[0:3, :], state[3:6, :], state[6:9, :], state[9:12, :]
        guess = jnp.concatenate(
            [
                xs + h * (v + h * (a / 2.0 + h * j / 6.0)),
                v + h * (a + h * j / 2.0),
            ],
            axis=0,
        )
        rows = jnp.where(first, state[0:6, :], guess)

        @pl.when(k >= 2)
        def _():
            wait_sent(par)

        send_swap(par, rows)
        set_target(rows)

        @pl.when(k < SUBSTEPS)
        def _():
            count = GB * LANES // SUBSTEPS

            def some(i, _):
                push(k * count + i * 16, lambda b, c: stars[b, c : c + 1, :])
                return 0

            lax.fori_loop(0, count // 16, some, 0)

        @pl.when(k == SUBSTEPS)
        def _():
            velocity = gvel[...] + HALF * pushed()
            bvel[...] = velocity
            moved = gpos[...] + STEP_TIME * velocity
            ogpos[...] = moved
            bodies[1, q] = jnp.concatenate([moved, body[...]], axis=0)
            send_bodies(1)
            widen(moved)

        fresh = rates(par, rows)
        a1, j1 = fresh[0:3], fresh[3:6]
        v1 = v + h / 2.0 * (a + a1) + h * h / 12.0 * (j - j1)
        x1 = xs + h / 2.0 * (v + v1) + h * h / 12.0 * (a - a1)
        state[0:3, :] = jnp.where(first, xs, x1)
        state[3:6, :] = jnp.where(first, v, v1)
        state[6:9, :] = a1
        state[9:12, :] = j1
        return 0

    lax.fori_loop(0, SUBSTEPS + 1, substep, 0)

    last = (SUBSTEPS + 1) % 2
    wait_sent(last)
    send_swap(last, state[0:6, :])
    set_position(state[0:3, :])
    for st in range(len(stages)):
        wait_bodies(1, stage_size[st], rb.at[1, st])
    pull_all(1)
    owned_out[...] = pulled()

    for gg in range(G):

        @pl.when((g != gg) | (z != g))
        def _():
            copy(owned_out, owned.at[z], so, ro, {"grp": gg, "sub": x * Z + g}).start()

    @pl.when(z == g)
    def _():
        owned[z] = owned_out[...]

    for st in range(len(stages)):
        wait_stage(last, st)
    opos[...] = swap[last, s, 0:3, :]

    def some_push(i, _):
        push(i * 16, lambda b, c: swap[last, b, c : c + 1, :])
        return 0

    lax.fori_loop(0, GB * LANES // 16, some_push, 0)
    ogvel[...] = bvel[...] + HALF * pushed()

    @pl.when(z == g)
    def _():
        wait_blocks(owned, Z - 1, ro)
        wait_blocks(owned, Z - 1, so)

    @pl.when(z != g)
    def _():
        wait_blocks(owned, Z, ro)
        wait_blocks(owned, Z, so)

    ovel[...] = swap[last, s, 3:6, :] + HALF * jnp.sum(owned[...], axis=0)[0:3]

    wait_blocks(stars, Z - 1, sa.at[0])
    wait_halves(sa.at[1])
    wait_blocks(ring, Z - 1, sz)
    for turn in range(2):
        wait_bodies(turn, NB - 1, sb.at[turn])
    wait_sent(1 - last)
    wait_sent(last)


def hand_on(*refs):
    for source, result in zip(refs[:4], refs[4:]):
        result[...] = source[...]


def solution(mesh):
    G = mesh.shape["grp"]
    NB = mesh.shape["sub"]
    Z = G
    X = NB // Z

    def local(cpos, cvel, cmass, gpos, gvel, gkind, species):
        bodies = gpos.shape[1]
        GB = bodies // LANES
        stages = len(chip_stages(X, G // 2))
        vmem = pl.BlockSpec(memory_space=pltpu.VMEM)
        smem = pl.BlockSpec(memory_space=pltpu.SMEM)
        dma = pltpu.SemaphoreType.DMA
        shapes = (
            jax.ShapeDtypeStruct(cpos.shape, F32),
            jax.ShapeDtypeStruct(cpos.shape, F32),
            jax.ShapeDtypeStruct(gpos.shape, F32),
            jax.ShapeDtypeStruct(gpos.shape, F32),
        )
        results = pl.pallas_call(
            functools.partial(kernel, (G, X, Z, NB, GB)),
            out_shape=shapes,
            in_specs=[vmem] * 6 + [smem],
            out_specs=(vmem,) * 4,
            scratch_shapes=[
                pltpu.VMEM((NB, 8, LANES), F32),
                pltpu.VMEM((3, bodies, LANES), F32),
                pltpu.VMEM((2, NB, 4, bodies), F32),
                pltpu.VMEM((Z, 4, LANES), F32),
                pltpu.VMEM((4, LANES), F32),
                pltpu.VMEM((2, NB, 8, LANES), F32),
                pltpu.VMEM((Z, 4, LANES), F32),
                pltpu.VMEM((4, LANES), F32),
                pltpu.VMEM((3, LANES, LANES), F32),
                pltpu.VMEM((LANES, 32), BF16),
                pltpu.VMEM((2, LANES, 4 * LANES), BF16),
                pltpu.VMEM((3, LANES, LANES), F32),
                pltpu.VMEM((LANES, 32), F32),
                pltpu.VMEM((3, bodies, LANES), F32),
                pltpu.VMEM((1, bodies), F32),
                pltpu.VMEM((3, bodies), F32),
                pltpu.VMEM((16, LANES), F32),
                dma((2,)), dma((2,)), dma((2,)), dma((2, stages)), dma, dma,
                dma((2,)), dma((2, stages)), dma, dma,
            ],
            compiler_params=pltpu.CompilerParams(collective_id=0, has_side_effects=True),
        )(cpos, cvel, cmass.reshape(1, LANES), gpos, gvel, gkind.reshape(1, bodies), species)
        return pl.pallas_call(
            hand_on, out_shape=shapes, in_specs=[vmem] * 4, out_specs=(vmem,) * 4
        )(*results)

    return jax.shard_map(
        local,
        mesh=mesh,
        in_specs=(
            P(None, "sub"),
            P(None, "sub"),
            P("sub"),
            P(None, ("grp", "sub")),
            P(None, ("grp", "sub")),
            P(("grp", "sub")),
            P(),
        ),
        out_specs=(
            P(None, "sub"),
            P(None, "sub"),
            P(None, ("grp", "sub")),
            P(None, ("grp", "sub")),
        ),
        check_vma=False,
    )
```

time: 141 us -> 107 us (0.76)
  Pallas kernels: 137 us -> 106 us
  local copies, waits for them, and re-layouts: 3.15 us -> 0 us
    pallas_call x1 -> x2, Pallas kernels: 137 us -> 106 us  [the longest x1 105 us: local(): pl.pallas_call(functools.partial(kernel, (G, X, Z, NB, GB)), out_shape=sh...]
    unnamed x10 -> x0, local copies, waits for them, and re-layouts: 3.15 us -> none
where the time goes in v3:
time: 107 us
  Pallas kernels  106 us (99%)
    pallas_call x1, Pallas kernels, local(): pl.pallas_call(functools.partial(kernel, (G, X, Z, NB, GB)), out_shape=sh...  105 us

profile of v3, /device:TPU:1, one launch (start us, length us, event | category | flops | bytes accessed | tf_op | source)
XLA Modules:
  0.0 106.7 jit_solution(9415565845841574361)
XLA Ops:
  0.6 104.7 %shard_map.102 = (f32[3,128]{1,0:T(4,128)}, f32[3,128]{1,0:T(4,128)}, f32[3,512]{1,0:T(4,128)}, f32[3,512]{1,0:T(4,128)}) custom-call(f32[3,128]{1,0:T(4,128)} %cpos.1, f32[3,128]{1,0:T(4,128)} %cvel.1, f32[1,128]{1,0:T(1,128)} %bitcast.3, f32[3,512]{1,0:T(4,128)} %gpos.1, f32[3,512]{1,0:T(4,128)} %gvel.1, s32[1,512]{1,0:T(1,128)} %bitcast.2, f32[4]{0:T(128)} %species.1), custom_call_target="tpu_custom_call" | custom-call | tf_op jit(solution)/shard_map/pallas_call | solution.py:501
  105.4 1.3 %shard_map.103 = (f32[3,128]{1,0:T(4,128)}, f32[3,128]{1,0:T(4,128)}, f32[3,512]{1,0:T(4,128)}, f32[3,512]{1,0:T(4,128)}) custom-call(f32[3,128]{1,0:T(4,128)} %get-tuple-element.8.refs_0_, f32[3,128]{1,0:T(4,128)} %get-tuple-element.9.refs_1_, f32[3,512]{1,0:T(4,128)} %get-tuple-element.10.refs_2_, f32[3,512]{1,0:T(4,128)} %get-tuple-element.11.refs_3_), custom_call_target="tpu_custom_call" | custom-call | tf_op jit(solution)/shard_map/pallas_call | solution.py:529

commit v4 on v3

--- a/solution.py
+++ b/solution.py
@@ -210,7 +210,7 @@
             def one(b, acc):
                 return pull(at, acc, [lanes_of(turn, b, l) for l in range(GB)])
 
-            return lax.fori_loop(0, NB, one, acc)
+            return lax.fori_loop(0, NB, one, acc, unroll=2)
 
         pull_rows(some, True)
 
@@ -222,7 +222,7 @@
         )
 
     def push(first, position_row):
-        here = pl.ds(pl.multiple_of(first, 16), 16)
+        here = pl.ds(pl.multiple_of(first, 32), 32)
         at = [wide[c, here, :] for c in range(3)]
 
         def step(b, acc):
@@ -232,7 +232,7 @@
             w = stars[b, 3:4, :] * (inv * inv * inv)
             return tuple(acc[c] + w * d[c] for c in range(3))
 
-        zero = jnp.zeros((16, LANES), F32)
+        zero = jnp.zeros((32, LANES), F32)
         acc = lax.fori_loop(0, NB, step, (zero, zero, zero), unroll=4)
         for c in range(3):
             accp[c, here, :] = acc[c]
@@ -306,7 +306,7 @@
         for c in range(3):
             target[c] = jnp.broadcast_to(cols[:, 32 + c : 33 + c], (LANES, LANES))
 
-    def rates_chip(par, chip, first, slot):
+    def rates_chip(par, chip, first, slot, base):
         sources, sums = [], []
         for k in range(2):
             tile = swap[par, chip + k]
@@ -343,23 +343,25 @@
                 w = inv * i2
                 mw = stars[b, 3:4, :] * w
                 acc = [acc[c] + mw * d[c] for c in range(3)]
-                weights[slot, here, lanes] = w.astype(BF16)
+                weights[slot, here, base + k * LANES : base + (k + 1) * LANES] = w.astype(BF16)
                 u = (w * i2) * rv[here, lanes]
-                weights[slot, here, 2 * LANES + k * LANES : 3 * LANES + k * LANES] = u.astype(BF16)
+                weights[slot, here, base + (2 + k) * LANES : base + (3 + k) * LANES] = u.astype(BF16)
             for c in range(3):
                 acc3[c, here, :] = acc[c]
-        out = lax.dot_general(
-            weights[slot], both, (((1,), (1,)), ((), ())), preferred_element_type=F32
-        )
-        accj[...] = out if first else accj[...] + out
+        return both
 
     def rates(par, rows):
-        turn = 0
         for st, chips in enumerate(stages):
             wait_stage(par, st)
-            for dx, dy in chips:
-                rates_chip(par, chip_at(dx, dy), turn == 0, turn % 2)
-                turn += 1
+            both = [
+                rates_chip(par, chip_at(dx, dy), st == 0, st % 2, i * 4 * LANES)
+                for i, (dx, dy) in enumerate(chips)
+            ]
+            out = lax.dot_general(
+                weights[st % 2, :, 0 : len(chips) * 4 * LANES], jnp.concatenate(both, axis=1),
+                (((1,), (1,)), ((), ())), preferred_element_type=F32,
+            )
+            accj[...] = out if st == 0 else accj[...] + out
         a = jnp.concatenate(
             [jnp.sum(acc3[c].T, axis=0, keepdims=True) for c in range(3)], axis=0
         )
@@ -396,10 +398,10 @@
             count = GB * LANES // SUBSTEPS
 
             def some(i, _):
-                push(k * count + i * 16, lambda b, c: stars[b, c : c + 1, :])
+                push(k * count + i * 32, lambda b, c: stars[b, c : c + 1, :])
                 return 0
 
-            lax.fori_loop(0, count // 16, some, 0)
+            lax.fori_loop(0, count // 32, some, 0)
 
         @pl.when(k == SUBSTEPS)
         def _():
@@ -447,10 +449,10 @@
     opos[...] = swap[last, s, 0:3, :]
 
     def some_push(i, _):
-        push(i * 16, lambda b, c: swap[last, b, c : c + 1, :])
+        push(i * 32, lambda b, c: swap[last, b, c : c + 1, :])
         return 0
 
-    lax.fori_loop(0, GB * LANES // 16, some_push, 0)
+    lax.fori_loop(0, GB * LANES // 32, some_push, 0)
     ogvel[...] = bvel[...] + HALF * pushed()
 
     @pl.when(z == g)
@@ -489,6 +491,7 @@
         bodies = gpos.shape[1]
         GB = bodies // LANES
         stages = len(chip_stages(X, G // 2))
+        longest = max(len(chips) for chips in chip_stages(X, G // 2))
         vmem = pl.BlockSpec(memory_space=pltpu.VMEM)
         smem = pl.BlockSpec(memory_space=pltpu.SMEM)
         dma = pltpu.SemaphoreType.DMA
@@ -514,7 +517,7 @@
                 pltpu.VMEM((4, LANES), F32),
                 pltpu.VMEM((3, LANES, LANES), F32),
                 pltpu.VMEM((LANES, 32), BF16),
-                pltpu.VMEM((2, LANES, 4 * LANES), BF16),
+                pltpu.VMEM((2, LANES, longest * 4 * LANES), BF16),
                 pltpu.VMEM((3, LANES, LANES), F32),
                 pltpu.VMEM((LANES, 32), F32),
                 pltpu.VMEM((3, bodies, LANES), F32),

time: 107 us -> 104 us (0.972)
  Pallas kernels: 106 us -> 103 us
    pallas_call x1, Pallas kernels: 105 us -> 102 us  [local(): pl.pallas_call(functools.partial(kernel, (G, X, Z, NB, GB)), out_shape=sh...]
where the time goes in v4:
time: 104 us; the launch traced here: 103 us
  Pallas kernels  103 us (99%)
    pallas_call x1, Pallas kernels, local(): pl.pallas_call(functools.partial(kernel, (G, X, Z, NB, GB)), out_shape=sh...  102 us

profile of v4, /device:TPU:1, one launch (start us, length us, event | category | flops | bytes accessed | tf_op | source)
XLA Modules:
  0.0 103.5 jit_solution(4954291593600458388)
XLA Ops:
  0.6 101.5 %shard_map.102 = (f32[3,128]{1,0:T(4,128)}, f32[3,128]{1,0:T(4,128)}, f32[3,512]{1,0:T(4,128)}, f32[3,512]{1,0:T(4,128)}) custom-call(f32[3,128]{1,0:T(4,128)} %cpos.1, f32[3,128]{1,0:T(4,128)} %cvel.1, f32[1,128]{1,0:T(1,128)} %bitcast.3, f32[3,512]{1,0:T(4,128)} %gpos.1, f32[3,512]{1,0:T(4,128)} %gvel.1, s32[1,512]{1,0:T(1,128)} %bitcast.2, f32[4]{0:T(128)} %species.1), custom_call_target="tpu_custom_call" | custom-call | tf_op jit(solution)/shard_map/pallas_call | solution.py:504
  102.2 1.3 %shard_map.103 = (f32[3,128]{1,0:T(4,128)}, f32[3,128]{1,0:T(4,128)}, f32[3,512]{1,0:T(4,128)}, f32[3,512]{1,0:T(4,128)}) custom-call(f32[3,128]{1,0:T(4,128)} %get-tuple-element.8.refs_0_, f32[3,128]{1,0:T(4,128)} %get-tuple-element.9.refs_1_, f32[3,512]{1,0:T(4,128)} %get-tuple-element.10.refs_2_, f32[3,512]{1,0:T(4,128)} %get-tuple-element.11.refs_3_), custom_call_target="tpu_custom_call" | custom-call | tf_op jit(solution)/shard_map/pallas_call | solution.py:532
